TPU v7x, 32 devices: a whole 2x2x4 slice. The times are simulated.
32 devices in a mesh: lat: 4 (over y, x), lon: 8 (over z, core).
Axes of the slice: x: 2, y: 2, z: 4, core: 2. Of those that a mesh axis runs over, the one named last changes fastest.
Arguments:
- fields: bfloat16 [1, 64, 64, 768], P(None, 'lat', 'lon'), may hold values from -6 to 6
- spec_cotangent: bfloat16 [2, 1, 64, 32, 768], P(None, None, 'lon', 'lat'), may hold values from -6 to 6
- inner_kernel: bfloat16 [2, 8, 96, 96], replicated, may hold values from -0.4375 to 0.4375
- inner_offset: float32 [2, 8, 96], replicated, may hold values from -3 to 3
- outer_kernel: bfloat16 [2, 8, 96, 96], replicated, may hold values from -0.4375 to 0.4375
- outer_offset: float32 [2, 8, 96], replicated, may hold values from -3 to 3
Outputs:
- filtered: float32 [2, 1, 64, 32, 768], P(None, None, 'lon', 'lat')
- inner_kernel_grad: float32 [2, 8, 96, 96], replicated
- inner_offset_grad: float32 [2, 8, 96], replicated
- outer_kernel_grad: float32 [2, 8, 96, 96], replicated
- outer_offset_grad: float32 [2, 8, 96], replicated
All inputs are finite; a program needn't handle non-finite values.
Results may differ from a plain program's by a relative error of at most 0.0072.
Values may be sent and summed in bfloat16 or wider, within the bound.
A program may use at most 64 MiB of HBM per device.

v0:
```python
import math
import jax
import jax.numpy as jnp
from jax import lax
from jax.sharding import PartitionSpec as P

shrink_level = 0.1
gelu_coeff = 0.7978845608028654
precise = lax.Precision.HIGHEST


def dft_tables(length, columns):
    points = jnp.arange(length, dtype=jnp.int32)
    orders = jnp.arange(columns, dtype=jnp.int32)
    product = points[:, None] * orders[None, :] % length
    angles = product.astype(jnp.float32) * (2.0 * math.pi / length)
    factor = 1.0 / math.sqrt(length)
    return (jnp.cos(angles) * factor, jnp.sin(angles) * factor)


def shrink(values):
    return values - shrink_level * jnp.tanh(values / shrink_level)


def shrink_slope(values):
    level = jnp.tanh(values / shrink_level)
    return level * level


def gelu_value(values):
    inner = gelu_coeff * (values + 0.044715 * values * values * values)
    return 0.5 * values * (1.0 + jnp.tanh(inner))


def gelu_slope(values):
    inner = gelu_coeff * (values + 0.044715 * values * values * values)
    level = jnp.tanh(inner)
    return 0.5 * (1.0 + level) + 0.5 * values * (1.0 - level * level) * gelu_coeff * (
        1.0 + 3.0 * 0.044715 * values * values
    )


def mixing(operand, kernel):
    return jnp.einsum("rnb,nbc->rnc", operand, kernel, preferred_element_type=jnp.float32)


def backmix(operand, kernel):
    return jnp.einsum("rnc,nbc->rnb", operand, kernel, preferred_element_type=jnp.float32)


def crossed(operand, second):
    return jnp.einsum("rnb,rnc->nbc", operand, second, preferred_element_type=jnp.float32)


def block_filter(spectrum, cotangent, inner_kernel, inner_offset, outer_kernel, outer_offset):
    spec_real, spec_imag = (spectrum[0], spectrum[1])
    pre_real = (
        mixing(spec_real, inner_kernel[0]) - mixing(spec_imag, inner_kernel[1]) + inner_offset[0]
    )
    pre_imag = (
        mixing(spec_imag, inner_kernel[0]) + mixing(spec_real, inner_kernel[1]) + inner_offset[1]
    )
    hid_real = gelu_value(pre_real).astype(jnp.bfloat16)
    hid_imag = gelu_value(pre_imag).astype(jnp.bfloat16)
    out_real = (
        mixing(hid_real, outer_kernel[0]) - mixing(hid_imag, outer_kernel[1]) + outer_offset[0]
    )
    out_imag = (
        mixing(hid_imag, outer_kernel[0]) + mixing(hid_real, outer_kernel[1]) + outer_offset[1]
    )
    filtered = jnp.stack([shrink(out_real), shrink(out_imag)])
    back_real = (cotangent[0].astype(jnp.float32) * shrink_slope(out_real)).astype(jnp.bfloat16)
    back_imag = (cotangent[1].astype(jnp.float32) * shrink_slope(out_imag)).astype(jnp.bfloat16)
    outer_grad = jnp.stack(
        [
            crossed(hid_real, back_real) + crossed(hid_imag, back_imag),
            crossed(hid_real, back_imag) - crossed(hid_imag, back_real),
        ]
    )
    outer_bias = jnp.stack(
        [
            jnp.sum(back_real, axis=0, dtype=jnp.float32),
            jnp.sum(back_imag, axis=0, dtype=jnp.float32),
        ]
    )
    grad_real = (
        (backmix(back_real, outer_kernel[0]) + backmix(back_imag, outer_kernel[1]))
        * gelu_slope(pre_real)
    ).astype(jnp.bfloat16)
    grad_imag = (
        (backmix(back_imag, outer_kernel[0]) - backmix(back_real, outer_kernel[1]))
        * gelu_slope(pre_imag)
    ).astype(jnp.bfloat16)
    inner_grad = jnp.stack(
        [
            crossed(spec_real, grad_real) + crossed(spec_imag, grad_imag),
            crossed(spec_real, grad_imag) - crossed(spec_imag, grad_real),
        ]
    )
    inner_bias = jnp.stack(
        [
            jnp.sum(grad_real, axis=0, dtype=jnp.float32),
            jnp.sum(grad_imag, axis=0, dtype=jnp.float32),
        ]
    )
    return (filtered, (inner_grad, inner_bias, outer_grad, outer_bias))


def per_device(fields, spec_cotangent, inner_kernel, inner_offset, outer_kernel, outer_offset):
    lat_devices = lax.axis_size("lat")
    lon_devices = lax.axis_size("lon")
    conditions = fields.shape[0]
    height = fields.shape[1] * lat_devices
    width = fields.shape[2] * lon_devices
    wavenumbers = width // 2
    cosine_rows, sine_rows = dft_tables(height, height)
    cosine_cols, sine_cols = dft_tables(width, wavenumbers)
    arriving = lax.all_to_all(fields, "lat", split_axis=3, concat_axis=1, tiled=True)
    shape_in = arriving.shape
    floats = arriving.astype(jnp.float32).reshape(
        shape_in[0], shape_in[1], shape_in[2] * shape_in[3]
    )
    real_part = jnp.einsum("bhx,hm->bmx", floats, cosine_rows, precision=precise)
    imag_part = -jnp.einsum("bhx,hm->bmx", floats, sine_rows, precision=precise)
    spec_rows = jnp.stack([real_part, imag_part]).reshape((2,) + shape_in)
    arriving = lax.all_to_all(spec_rows, "lon", split_axis=2, concat_axis=3, tiled=True)
    real_part = jnp.einsum(
        "bhwd,wk->bhkd", arriving[0], cosine_cols, precision=precise
    ) + jnp.einsum("bhwd,wk->bhkd", arriving[1], sine_cols, precision=precise)
    imag_part = jnp.einsum(
        "bhwd,wk->bhkd", arriving[1], cosine_cols, precision=precise
    ) - jnp.einsum("bhwd,wk->bhkd", arriving[0], sine_cols, precision=precise)
    spec_half = jnp.stack([real_part, imag_part]).astype(jnp.bfloat16)
    spectrum = lax.all_to_all(spec_half, "lat", split_axis=3, concat_axis=4, tiled=True)
    blocks = inner_kernel.shape[1]
    block_width = inner_kernel.shape[2]
    local_shape = spectrum.shape
    flat_spec = spectrum.reshape(2, -1, blocks, block_width)
    flat_cot = spec_cotangent.reshape(2, -1, blocks, block_width)
    filtered, gradients = block_filter(
        flat_spec, flat_cot, inner_kernel, inner_offset, outer_kernel, outer_offset
    )
    totals = lax.psum((gradients[0], gradients[1], gradients[2], gradients[3]), ("lat", "lon"))
    normalizer = 1.0 / math.sqrt(conditions * height * wavenumbers)
    return (
        filtered.reshape(local_shape),
        totals[0] * normalizer,
        totals[1] * normalizer,
        totals[2] * normalizer,
        totals[3] * normalizer,
    )


def solution(mesh):
    placed = (P(None, "lat", "lon", None), P(None, None, "lon", "lat", None), P(), P(), P(), P())
    return jax.shard_map(
        per_device,
        mesh=mesh,
        in_specs=placed,
        out_specs=(P(None, None, "lon", "lat", None), P(), P(), P(), P()),
        check_vma=False,
    )
```

profile of v0, /device:TPU:0, one launch (start us, length us, event | category | flops | bytes accessed | tf_op | source)
XLA Modules:
  0.0 218.2 jit_solution(6437234970947821318)
XLA Ops:
  7.2 2.2 copy.51
  9.3 1.6 reshape.124
  10.9 10.5 %all_to_all.45 = bf16[4,2,12288]{2,1,0:T(2,128)(2,1)S(1)} all-to-all(bf16[4,2,12288]{2,1,0:T(2,128)(2,1)S(1)} %reshape.124), channel_id=1, replica_groups=mesh['lat'=4,'lon'=8] {'lat'}, dimensions={0} | all-to-all | bytes 393216 | tf_op jit(solution)/shard_map/all_to_all | solution.py:118
  21.4 1.2 reshape.125
  22.6 1.0 copy.52
  23.6 0.2 reshape.116
  23.9 0.4 convolution_negate_fusion
  24.3 0.2 dot_general.85
  24.5 0.5 convolution_bitcast_fusion
  25.0 0.2 stack.60
  25.2 0.2 copy.54
  25.4 0.1 pad_maximum_fusion
  25.5 1.6 copy.55
  27.1 5.0 %all-to-all-start.1 = ((f32[2,1,64,8,192]{4,3,1,0,2:T(8,128)}), f32[2,1,64,8,192]{4,3,1,0,2:T(8,128)S(1)}, u32[]{:S(2)}, u32[]{:S(2)}) async-start(f32[2,1,64,8,192]{4,3,1,0,2:T(8,128)} %copy.55), calls=%async_computation.1 | async-start | bytes 2097152 | tf_op jit(solution)/shard_map/all_to_all | solution.py:126
  32.1 0.1 reshape.119
  32.2 0.1 reshape.120
  32.4 26.3 %all-to-all-done.1 = f32[2,1,64,8,192]{4,3,1,0,2:T(8,128)S(1)} async-done(((f32[2,1,64,8,192]{4,3,1,0,2:T(8,128)}), f32[2,1,64,8,192]{4,3,1,0,2:T(8,128)S(1)}, u32[]{:S(2)}, u32[]{:S(2)}) %all-to-all-start.1) | async-done | bytes 786464 | tf_op jit(solution)/shard_map/all_to_all | solution.py:126
  58.7 0.1 copy.103
  58.8 0.5 fusion.23
  59.2 0.5 fusion.22
  59.7 0.0 copy-start.4
  59.7 0.5 fusion.20
  60.2 0.5 fusion.21
  60.6 0.0 copy-start.1
  60.7 0.9 copy.57
  61.6 3.4 %all-to-all-start.2 = ((bf16[2,1,8,32,192]{4,2,1,0,3:T(8,128)(2,1)}), bf16[2,1,8,32,192]{4,2,1,0,3:T(8,128)(2,1)S(1)}, u32[]{:S(2)}, u32[]{:S(2)}) async-start(bf16[2,1,8,32,192]{4,2,1,0,3:T(8,128)(2,1)} %copy.57), calls=%async_computation.2 | async-start | bytes 524288 | tf_op jit(solution)/shard_map/all_to_all | solution.py:134
  65.0 0.2 all-reduce.4.cloned.1.call-start
  65.2 5.2 %all-to-all-done.2 = bf16[2,1,8,32,192]{4,2,1,0,3:T(8,128)(2,1)S(1)} async-done(((bf16[2,1,8,32,192]{4,2,1,0,3:T(8,128)(2,1)}), bf16[2,1,8,32,192]{4,2,1,0,3:T(8,128)(2,1)S(1)}, u32[]{:S(2)}, u32[]{:S(2)}) %all-to-all-start.2) | async-done | bytes 196640 | tf_op jit(solution)/shard_map/all_to_all | solution.py:134
  70.4 0.2 copy.104
  70.6 0.1 fusion.142
  70.7 0.1 squeeze.12
  70.9 0.1 squeeze.14
  71.0 0.2 fusion.51
  71.2 0.2 fusion.53
  71.4 0.3 multiply_convert_fusion
  71.7 0.2 fusion.45
  71.9 0.3 multiply_convert_fusion.1
  72.1 0.2 fusion.47
  72.3 0.3 convert_reduce_fusion.1
  72.6 0.2 fusion.43
  72.8 0.3 fusion.143
  73.1 0.3 convert_reduce_fusion
  73.4 0.2 fusion.41
  73.6 0.3 fusion.144
  73.9 0.3 convert_reduce_fusion.3
  74.2 0.2 fusion.73
  74.5 0.3 convert_reduce_fusion.2
  74.8 0.2 fusion.71
  75.0 0.3 fusion.3
  75.3 0.3 fusion.2
  75.5 0.3 fusion.1
  75.8 0.3 fusion
  76.1 0.9 pad_maximum_fusion.1
  77.0 0.9 pad_maximum_fusion.2
  78.0 0.0 all-reduce.4.cloned.1.call-update
  78.0 0.2 copy.64
  78.2 0.1 stack.66
  78.3 0.2 copy.63
  78.4 0.1 stack.65
  78.6 37.5 %all-reduce = (f32[2,8,96]{2,1,0:T(8,128)S(1)}, f32[2,8,96]{2,1,0:T(8,128)S(1)}) all-reduce(f32[2,8,96]{2,1,0:T(8,128)S(1)} %pad_maximum_fusion.5, f32[2,8,96]{2,1,0:T(8,128)S(1)} %pad_maximum_fusion.6), channel_id=1, replica_groups=mesh['lat'=4,'lon'=8] {'lat','lon'}, use_global_device_ids=true, to_apply=%region_3.4 | all-reduce | flops 3072 | bytes 24576 | tf_op jit(solution)/shard_map/psum | solution.py:143
  116.1 0.8 pad_maximum_fusion.3
  116.9 0.6 broadcast_multiply_fusion.2
  117.5 91.3 %all-reduce.4.cloned.1.call-done = (f32[2,8,96,96]{3,2,1,0:T(8,128)}, f32[2,8,96,96]{3,2,1,0:T(8,128)}) async-done(((f32[2,8,96,96]{3,2,1,0:T(8,128)}, f32[2,8,96,96]{3,2,1,0:T(8,128)}), (f32[2,8,96,96]{3,2,1,0:T(8,128)}, f32[2,8,96,96]{3,2,1,0:T(8,128)})) %all-reduce.4.cloned.1.call-update) | async-done | bytes 1179664 | tf_op jit(solution)/shard_map/psum | solution.py:143
  208.7 2.7 %broadcast_multiply_fusion = (f32[2,8,96,96]{3,2,1,0:T(8,128)}, f32[2,8,96,96]{3,2,1,0:T(8,128)}) fusion(f32[2,8,96,96]{3,2,1,0:T(8,128)} %get-tuple-element.8, f32[2,8,96,96]{3,2,1,0:T(8,128)} %get-tuple-element.7), kind=kLoop, calls=%fused_computation.45 | loop fusion | flops 294912 | bytes 2359296 | tf_op jit(solution)/shard_map/mul | solution.py:149
  (14 shorter events, 0.1 us)
Async XLA Ops:
  27.0 5.0 %copy-start.2 = (bf16[2,1,8,8,768]{4,3,2,1,0:T(8,128)(2,1)S(1)}, bf16[2,1,8,8,768]{4,3,2,1,0:T(8,128)(2,1)}, u32[]{:S(2)}) copy-start(bf16[2,1,8,8,768]{4,3,2,1,0:T(8,128)(2,1)} %param.7) | copy-start | bytes 589828
  27.1 5.3 %copy-start.3 = (f32[2,8,96]{2,1,0:T(8,128)S(1)}, f32[2,8,96]{2,1,0:T(8,128)}, u32[]{:S(2)}) copy-start(f32[2,8,96]{2,1,0:T(8,128)} %param.9) | copy-start | bytes 18436
  27.1 31.6 %all-to-all-start.1 = ((f32[2,1,64,8,192]{4,3,1,0,2:T(8,128)}), f32[2,1,64,8,192]{4,3,1,0,2:T(8,128)S(1)}, u32[]{:S(2)}, u32[]{:S(2)}) async-start(f32[2,1,64,8,192]{4,3,1,0,2:T(8,128)} %copy.55), calls=%async_computation.1 | async-start | bytes 2097152 | tf_op jit(solution)/shard_map/all_to_all | solution.py:126
  59.7 5.5 %copy-start.4 = (f32[2,8,96]{2,1,0:T(8,128)S(1)}, f32[2,8,96]{2,1,0:T(8,128)}, u32[]{:S(2)}) copy-start(f32[2,8,96]{2,1,0:T(8,128)} %param.11) | copy-start | bytes 18436
  60.6 10.4 %copy-start.1 = (bf16[2,8,96,96]{3,2,1,0:T(8,128)(2,1)S(1)}, bf16[2,8,96,96]{3,2,1,0:T(8,128)(2,1)}, u32[]{:S(2)}) copy-start(bf16[2,8,96,96]{3,2,1,0:T(8,128)(2,1)} %param.8) | copy-start | bytes 884740
  61.6 8.8 %all-to-all-start.2 = ((bf16[2,1,8,32,192]{4,2,1,0,3:T(8,128)(2,1)}), bf16[2,1,8,32,192]{4,2,1,0,3:T(8,128)(2,1)S(1)}, u32[]{:S(2)}, u32[]{:S(2)}) async-start(bf16[2,1,8,32,192]{4,2,1,0,3:T(8,128)(2,1)} %copy.57), calls=%async_computation.2 | async-start | bytes 524288 | tf_op jit(solution)/shard_map/all_to_all | solution.py:134
  65.0 143.8 %all-reduce.4.cloned.1.call-start = ((), (), s32[]{:S(2)}) async-start(), calls=%async_computation.3 | async-start | bytes 3145728 | tf_op jit(solution)/shard_map/psum | solution.py:143
  70.6 1.1 copy-start
Sparse Core Ops, SparseCore 0:
  78.1 130.5 all-reduce.3
where the time goes:
time: 219 us; the launch traced here: 218 us
  waiting for transfers between devices  123 us (56%)
  blocking collectives  48 us (22%)
  between operations  14.4 us (7%)
  local copies, waits for them, and re-layouts  10.7 us (5%)
  starting transfers between devices  8.63 us (4%)
  matrix products  7.71 us (4%)
  other arithmetic  6.09 us (3%)
    psum x1, waiting for transfers between devices, per_device(): lax.psum((gradients[0], gradients[1], gradients[2], gradients[3]), ('lat'...  91.3 us
    psum x1, blocking collectives, per_device(): lax.psum((gradients[0], gradients[1], gradients[2], gradients[3]), ('lat'...  37.5 us
    all_to_all x1, waiting for transfers between devices, per_device(): lax.all_to_all(spec_rows, 'lon', split_axis=2, concat_axis=3, tiled=True)  26.3 us
    all_to_all x1, blocking collectives, per_device(): lax.all_to_all(fields, 'lat', split_axis=3, concat_axis=1, tiled=True)  10.5 us
    all_to_all x1, waiting for transfers between devices, per_device(): lax.all_to_all(spec_half, 'lat', split_axis=3, concat_axis=4, tiled=True)  5.17 us
    all_to_all x1, starting transfers between devices, per_device(): lax.all_to_all(spec_rows, 'lon', split_axis=2, concat_axis=3, tiled=True)  5 us
    unnamed x13, local copies, waits for them, and re-layouts  4.92 us
  transfers between devices with their start and end apart: 3, of which 3 were waited for; matrix products, arithmetic and copies ran while one was open for 1% of the time, Pallas kernels for 0%

commit v1 on v0

--- a/solution.py
+++ b/solution.py
@@ -140,7 +140,9 @@
     filtered, gradients = block_filter(
         flat_spec, flat_cot, inner_kernel, inner_offset, outer_kernel, outer_offset
     )
-    totals = lax.psum((gradients[0], gradients[1], gradients[2], gradients[3]), ("lat", "lon"))
+    totals = lax.psum(
+        lax.psum((gradients[0], gradients[1], gradients[2], gradients[3]), "lon"), "lat"
+    )
     normalizer = 1.0 / math.sqrt(conditions * height * wavenumbers)
     return (
         filtered.reshape(local_shape),

time: 219 us -> 212 us (0.968)
  waiting for transfers between devices: 123 us -> 111 us
  blocking collectives: 48 us -> 52.5 us
    psum x1 -> x2, waiting for transfers between devices: 91.3 us -> 79.3 us  [the longest x1 60.2 us: per_device(): lax.psum((gradients[0], gradients[1], gradients[2], gradients[3]), 'lon')]
    psum x1 -> x2, blocking collectives: 37.5 us -> 42 us  [the longest x1 25.9 us: per_device(): lax.psum((gradients[0], gradients[1], gradients[2], gradients[3]), 'lon')]
    mul x0 -> x2, other arithmetic: none -> 2.76 us  [the longest x1 2.16 us: per_device(): totals[0] * normalizer]
    unnamed x13 -> x15, local copies, waits for them, and re-layouts: 4.92 us -> 4.93 us
  transfers between devices with their start and end apart: 3 -> 4, of which waited for: 3 -> 4; matrix products, arithmetic and copies ran while one was open for 1% -> 1% of each run, Pallas kernels for 0% -> 0%
where the time goes in v1:
time: 212 us; the launch traced here: 211 us
  waiting for transfers between devices  111 us (52%)
  blocking collectives  52.5 us (25%)
  between operations  14.4 us (7%)
  local copies, waits for them, and re-layouts  10.7 us (5%)
  starting transfers between devices  8.67 us (4%)
  matrix products  7.72 us (4%)
  other arithmetic  6.54 us (3%)
    psum x1, waiting for transfers between devices, per_device(): lax.psum((gradients[0], gradients[1], gradients[2], gradients[3]), 'lon')  60.2 us
    all_to_all x1, waiting for transfers between devices, per_device(): lax.all_to_all(spec_rows, 'lon', split_axis=2, concat_axis=3, tiled=True)  26.3 us
    psum x1, blocking collectives, per_device(): lax.psum((gradients[0], gradients[1], gradients[2], gradients[3]), 'lon')  25.9 us
    psum x1, waiting for transfers between devices, per_device(): lax.psum(lax.psum((gradients[0], gradients[1], gradients[2], gradients[3]...  19.1 us
    psum x1, blocking collectives, per_device(): lax.psum(lax.psum((gradients[0], gradients[1], gradients[2], gradients[3]...  16.1 us
    all_to_all x1, blocking collectives, per_device(): lax.all_to_all(fields, 'lat', split_axis=3, concat_axis=1, tiled=True)  10.5 us
    all_to_all x1, waiting for transfers between devices, per_device(): lax.all_to_all(spec_half, 'lat', split_axis=3, concat_axis=4, tiled=True)  5.15 us
    all_to_all x1, starting transfers between devices, per_device(): lax.all_to_all(spec_rows, 'lon', split_axis=2, concat_axis=3, tiled=True)  5 us
  transfers between devices with their start and end apart: 4, of which 4 were waited for; matrix products, arithmetic and copies ran while one was open for 1% of the time, Pallas kernels for 0%

profile of v1, /device:TPU:0, one launch (start us, length us, event | category | flops | bytes accessed | tf_op | source)
XLA Modules:
  0.0 211.3 jit_solution(12195307395256194388)
XLA Ops:
  7.2 2.2 %copy.51 = bf16[1,16,8,768]{1,2,0,3:T(8,128)(2,1)S(1)} copy(bf16[1,16,8,768]{3,2,1,0:T(8,128)(2,1)} %param.6) | data formatting | bytes 393216 | tf_op args[0]
  9.3 1.6 reshape.124
  10.9 10.5 %all_to_all.45 = bf16[4,2,12288]{2,1,0:T(2,128)(2,1)S(1)} all-to-all(bf16[4,2,12288]{2,1,0:T(2,128)(2,1)S(1)} %reshape.124), channel_id=1, replica_groups=mesh['lat'=4,'lon'=8] {'lat'}, dimensions={0} | all-to-all | bytes 393216 | tf_op jit(solution)/shard_map/all_to_all | solution.py:118
  21.4 1.2 reshape.125
  22.6 1.0 copy.52
  23.6 0.2 reshape.116
  23.9 0.4 convolution_negate_fusion
  24.3 0.2 dot_general.85
  24.5 0.5 convolution_bitcast_fusion
  25.0 0.2 stack.60
  25.2 0.2 copy.54
  25.4 0.1 pad_maximum_fusion
  25.5 1.6 copy.55
  27.1 5.0 %all-to-all-start.1 = ((f32[2,1,64,8,192]{4,3,1,0,2:T(8,128)}), f32[2,1,64,8,192]{4,3,1,0,2:T(8,128)S(1)}, u32[]{:S(2)}, u32[]{:S(2)}) async-start(f32[2,1,64,8,192]{4,3,1,0,2:T(8,128)} %copy.55), calls=%async_computation.1 | async-start | bytes 2097152 | tf_op jit(solution)/shard_map/all_to_all | solution.py:126
  32.1 0.1 reshape.119
  32.3 0.1 reshape.120
  32.4 26.3 %all-to-all-done.1 = f32[2,1,64,8,192]{4,3,1,0,2:T(8,128)S(1)} async-done(((f32[2,1,64,8,192]{4,3,1,0,2:T(8,128)}), f32[2,1,64,8,192]{4,3,1,0,2:T(8,128)S(1)}, u32[]{:S(2)}, u32[]{:S(2)}) %all-to-all-start.1) | async-done | bytes 786464 | tf_op jit(solution)/shard_map/all_to_all | solution.py:126
  58.7 0.1 copy.103
  58.8 0.5 fusion.23
  59.2 0.5 fusion.22
  59.7 0.5 fusion.20
  60.2 0.5 fusion.21
  60.7 0.9 copy.57
  61.6 3.4 %all-to-all-start.2 = ((bf16[2,1,8,32,192]{4,2,1,0,3:T(8,128)(2,1)}), bf16[2,1,8,32,192]{4,2,1,0,3:T(8,128)(2,1)S(1)}, u32[]{:S(2)}, u32[]{:S(2)}) async-start(bf16[2,1,8,32,192]{4,2,1,0,3:T(8,128)(2,1)} %copy.57), calls=%async_computation.2 | async-start | bytes 524288 | tf_op jit(solution)/shard_map/all_to_all | solution.py:134
  65.0 0.2 all-reduce.7.cloned.1.call-start
  65.3 5.1 %all-to-all-done.2 = bf16[2,1,8,32,192]{4,2,1,0,3:T(8,128)(2,1)S(1)} async-done(((bf16[2,1,8,32,192]{4,2,1,0,3:T(8,128)(2,1)}), bf16[2,1,8,32,192]{4,2,1,0,3:T(8,128)(2,1)S(1)}, u32[]{:S(2)}, u32[]{:S(2)}) %all-to-all-start.2) | async-done | bytes 196640 | tf_op jit(solution)/shard_map/all_to_all | solution.py:134
  70.4 0.2 copy.104
  70.6 0.1 fusion.142
  70.7 0.1 squeeze.12
  70.9 0.1 squeeze.14
  71.0 0.2 fusion.51
  71.2 0.2 fusion.53
  71.4 0.3 multiply_convert_fusion
  71.7 0.2 fusion.45
  71.9 0.3 multiply_convert_fusion.1
  72.1 0.2 fusion.47
  72.3 0.3 convert_reduce_fusion.1
  72.6 0.2 fusion.43
  72.8 0.3 fusion.143
  73.1 0.3 convert_reduce_fusion
  73.4 0.2 fusion.41
  73.6 0.3 fusion.144
  73.9 0.3 convert_reduce_fusion.3
  74.2 0.2 fusion.73
  74.5 0.3 convert_reduce_fusion.2
  74.8 0.2 fusion.71
  75.0 0.3 fusion.3
  75.3 0.3 fusion.2
  75.5 0.3 fusion.1
  75.8 0.3 fusion
  76.1 1.3 pad_maximum_fusion.1
  77.4 60.2 %all-reduce.7.cloned.1.call-done = (f32[2,8,96,96]{3,2,1,0:T(8,128)}, f32[2,8,96,96]{3,2,1,0:T(8,128)}) async-done(((f32[2,8,96,96]{3,2,1,0:T(8,128)}, f32[2,8,96,96]{3,2,1,0:T(8,128)}), (f32[2,8,96,96]{3,2,1,0:T(8,128)}, f32[2,8,96,96]{3,2,1,0:T(8,128)})) %all-reduce.7.cloned.1.call-update) | async-done | bytes 1179664 | tf_op jit(solution)/shard_map/psum | solution.py:144
  137.7 0.2 copy.64
  137.8 0.1 stack.66
  138.0 0.2 copy.63
  138.1 0.1 stack.65
  138.3 25.9 %all-reduce = (f32[2,8,96]{2,1,0:T(8,128)S(1)}, f32[2,8,96]{2,1,0:T(8,128)S(1)}) all-reduce(f32[2,8,96]{2,1,0:T(8,128)S(1)} %get-tuple-element.37, f32[2,8,96]{2,1,0:T(8,128)S(1)} %get-tuple-element.38), channel_id=1, replica_groups=mesh['lat'=4,'lon'=8] {'lon'}, use_global_device_ids=true, to_apply=%region_4.5 | all-reduce | flops 3072 | bytes 24576 | tf_op jit(solution)/shard_map/psum | solution.py:144
  164.2 16.1 %all-reduce.2 = (f32[2,8,96]{2,1,0:T(8,128)S(1)}, f32[2,8,96]{2,1,0:T(8,128)S(1)}) all-reduce(f32[2,8,96]{2,1,0:T(8,128)S(1)} %get-tuple-element.5, f32[2,8,96]{2,1,0:T(8,128)S(1)} %get-tuple-element.6), channel_id=1, replica_groups=mesh['lat'=4,'lon'=8] {'lat'}, use_global_device_ids=true, to_apply=%region_5.6 | all-reduce | flops 3072 | bytes 24576 | tf_op jit(solution)/shard_map/psum | solution.py:143
  180.3 0.8 pad_maximum_fusion.3
  181.1 0.6 broadcast_multiply_fusion.3
  181.7 0.6 broadcast_multiply_fusion.2
  182.3 19.1 %all-reduce.9.cloned.1.call-done = (f32[2,8,96,96]{3,2,1,0:T(8,128)}, f32[2,8,96,96]{3,2,1,0:T(8,128)}) async-done(((f32[2,8,96,96]{3,2,1,0:T(8,128)}, f32[2,8,96,96]{3,2,1,0:T(8,128)}), (f32[2,8,96,96]{3,2,1,0:T(8,128)}, f32[2,8,96,96]{3,2,1,0:T(8,128)})) %all-reduce.9.cloned.1.call-update) | async-done | bytes 1179664 | tf_op jit(solution)/shard_map/psum | solution.py:143
  201.4 2.2 %broadcast_multiply_fusion.1 = f32[2,8,96,96]{3,2,1,0:T(8,128)} fusion(f32[2,8,96,96]{3,2,1,0:T(8,128)} %get-tuple-element.11), kind=kLoop, calls=%fused_computation.46 | loop fusion | flops 147456 | bytes 1179648 | tf_op jit(solution)/shard_map/mul | solution.py:149
  203.5 1.0 broadcast_multiply_fusion
  (20 shorter events, 0.2 us)
Async XLA Ops:
  27.1 5.0 %copy-start.3 = (bf16[2,1,8,8,768]{4,3,2,1,0:T(8,128)(2,1)S(1)}, bf16[2,1,8,8,768]{4,3,2,1,0:T(8,128)(2,1)}, u32[]{:S(2)}) copy-start(bf16[2,1,8,8,768]{4,3,2,1,0:T(8,128)(2,1)} %param.7) | copy-start | bytes 589828
  27.1 5.3 %copy-start.4 = (f32[2,8,96]{2,1,0:T(8,128)S(1)}, f32[2,8,96]{2,1,0:T(8,128)}, u32[]{:S(2)}) copy-start(f32[2,8,96]{2,1,0:T(8,128)} %param.9) | copy-start | bytes 18436
  27.1 31.6 %all-to-all-start.1 = ((f32[2,1,64,8,192]{4,3,1,0,2:T(8,128)}), f32[2,1,64,8,192]{4,3,1,0,2:T(8,128)S(1)}, u32[]{:S(2)}, u32[]{:S(2)}) async-start(f32[2,1,64,8,192]{4,3,1,0,2:T(8,128)} %copy.55), calls=%async_computation.1 | async-start | bytes 2097152 | tf_op jit(solution)/shard_map/all_to_all | solution.py:126
  59.7 5.5 %copy-start.5 = (f32[2,8,96]{2,1,0:T(8,128)S(1)}, f32[2,8,96]{2,1,0:T(8,128)}, u32[]{:S(2)}) copy-start(f32[2,8,96]{2,1,0:T(8,128)} %param.11) | copy-start | bytes 18436
  60.7 10.4 %copy-start.2 = (bf16[2,8,96,96]{3,2,1,0:T(8,128)(2,1)S(1)}, bf16[2,8,96,96]{3,2,1,0:T(8,128)(2,1)}, u32[]{:S(2)}) copy-start(bf16[2,8,96,96]{3,2,1,0:T(8,128)(2,1)} %param.8) | copy-start | bytes 884740
  61.6 8.8 %all-to-all-start.2 = ((bf16[2,1,8,32,192]{4,2,1,0,3:T(8,128)(2,1)}), bf16[2,1,8,32,192]{4,2,1,0,3:T(8,128)(2,1)S(1)}, u32[]{:S(2)}, u32[]{:S(2)}) async-start(bf16[2,1,8,32,192]{4,2,1,0,3:T(8,128)(2,1)} %copy.57), calls=%async_computation.2 | async-start | bytes 524288 | tf_op jit(solution)/shard_map/all_to_all | solution.py:134
  65.0 72.6 %all-reduce.7.cloned.1.call-start = ((), (), s32[]{:S(2)}) async-start(), calls=%async_computation.3 | async-start | bytes 3145728 | tf_op jit(solution)/shard_map/psum | solution.py:144
  70.6 1.1 copy-start
  77.4 124.0 %all-reduce.9.cloned.1.call-start = ((), (), s32[]{:S(2)}) async-start(), calls=%async_computation.4 | async-start | bytes 3145728 | tf_op jit(solution)/shard_map/psum | solution.py:143
  201.4 2.2 %copy-start.1 = (f32[2,8,96,96]{3,2,1,0:T(8,128)S(1)}, f32[2,8,96,96]{3,2,1,0:T(8,128)}, u32[]{:S(2)}) copy-start(f32[2,8,96,96]{3,2,1,0:T(8,128)} %get-tuple-element.12) | copy-start | bytes 1769476
Sparse Core Ops, SparseCore 0:
  77.5 60.0 all-reduce.6
  140.7 60.5 all-reduce.8
